TPU v7x, 512 devices: a whole 4x4x16 slice. The times are simulated.
512 devices in a mesh: ep: 64 (over x_lo, z, core), blk: 8 (over x_hi, y).
Axes of the slice: x: 4 (x_hi: 2, x_lo: 2; x = x_hi * 2 + x_lo), y: 4, z: 16, core: 2. Of those that a mesh axis runs over, the one named last changes fastest.
Arguments:
- tokens: bfloat16 [4096, 2048], P(('ep', 'blk')), may hold values from -6 to 6
- routes: int32 [4096, 8], P('ep'), may hold values from 0 to 63, all different within a row; in each aligned block of 64 rows (0 to 63, 64 to 127, ...) at most 16 rows name the same one
- gate_scale: bfloat16 [4096, 8], P('ep'), may hold values from 0.099609375 to 1
- placement: int32 [64], replicated, may hold values from 0 to 63, each once
- w_gate: bfloat16 [64, 2048, 1024], P('ep', None, 'blk'), may hold values from -0.125 to 0.125
- w_up: bfloat16 [64, 2048, 1024], P('ep', None, 'blk'), may hold values from -0.125 to 0.125
- w_down: bfloat16 [64, 1024, 2048], P('ep', 'blk'), may hold values from -0.1875 to 0.1875
Outputs:
- mixed: bfloat16 [4096, 2048], P(('ep', 'blk'))
Inputs may be any that keep to these rules, and one draw needn't show every extreme that they name: `routes`: in each aligned block of 64 rows (the tokens of one index of ep) no expert is named by more than 16 rows, a bound that some block reaches; a row names 8 different experts. `placement`: each ep index holds exactly one expert.
All inputs are finite; a program needn't handle non-finite values.
Results may differ from a plain program's by a relative error of at most 0.019.
Values may be sent and summed in bfloat16 or wider, within the bound.
A program may use at most 64 MiB of HBM per device.

v0:
```python
import jax
import jax.numpy as jnp
from jax import lax
from jax.sharding import PartitionSpec as P

TOP = 8


def expert_rows(arrived, w_gate, w_up, w_down):
    row_shape = arrived.shape
    flat_rows = arrived.reshape(-1, row_shape[-1])
    gate_proj = jnp.dot(flat_rows, w_gate[0], preferred_element_type=jnp.float32)
    up_proj = jnp.dot(flat_rows, w_up[0], preferred_element_type=jnp.float32)
    hidden = (jax.nn.silu(gate_proj) * up_proj).astype(jnp.bfloat16)
    output = jnp.dot(hidden, w_down[0], preferred_element_type=jnp.float32).astype(jnp.bfloat16)
    return output.reshape(row_shape)


def local(tokens, routes, gate_scale, placement, w_gate, w_up, w_down):
    ep_count = lax.axis_size("ep")
    blk_count = lax.axis_size("blk")
    own_count = tokens.shape[0]
    width = tokens.shape[1]
    block_size = own_count * blk_count
    capacity = blk_count * max(1, 2 * TOP * own_count // ep_count)
    slots_total = ep_count * capacity
    gathered = lax.all_gather(tokens, "blk", axis=0, tiled=True)
    ep_ids = lax.iota(jnp.int32, ep_count)
    holder = jnp.sum(
        jnp.where(routes[:, :, None] == ep_ids[None, None, :], placement[None, None, :], 0), axis=-1
    )
    flat_holder = holder.reshape(-1)
    onehot = (flat_holder[:, None] == ep_ids[None, :]).astype(jnp.int32)
    before = jnp.cumsum(onehot, axis=0) - onehot
    slot_index = jnp.sum(before * onehot, axis=1)
    position = flat_holder * capacity + slot_index
    matches = (position[None, :] == lax.iota(jnp.int32, slots_total)[:, None]).reshape(
        slots_total, block_size, TOP
    )
    picked = jnp.any(matches, axis=2).astype(jnp.bfloat16)
    buffer = jnp.dot(picked, gathered, preferred_element_type=jnp.float32).astype(jnp.bfloat16)
    buffer = buffer.reshape(ep_count, capacity, width)
    combine_weights = jnp.sum(
        jnp.where(matches, gate_scale[None, :, :], jnp.zeros((), jnp.bfloat16)), axis=2
    )
    finished = None
    arrived = lax.all_to_all(buffer, "ep", split_axis=0, concat_axis=0, tiled=True)
    returned = lax.all_to_all(
        expert_rows(arrived, w_gate, w_up, w_down), "ep", split_axis=0, concat_axis=0, tiled=True
    )
    returned_flat = returned.reshape(slots_total, width)
    combined = lax.dot_general(
        combine_weights, returned_flat, (((0,), (0,)), ((), ())), preferred_element_type=jnp.float32
    )
    summed = lax.psum_scatter(combined.astype(jnp.bfloat16), "blk", scatter_dimension=0, tiled=True)
    finished = summed
    return finished


def solution(mesh):
    in_specs = (
        P(("ep", "blk"), None),
        P("ep", None),
        P("ep", None),
        P(),
        P("ep", None, "blk"),
        P("ep", None, "blk"),
        P("ep", "blk", None),
    )
    out_specs = P(("ep", "blk"), None)
    return jax.shard_map(local, mesh=mesh, in_specs=in_specs, out_specs=out_specs, check_vma=False)
```

profile of v0, /device:TPU:32, one launch (start us, length us, event | category | flops | bytes accessed | tf_op | source)
XLA Modules:
  0.0 550.5 jit_solution(13190970564214001270)
XLA Ops:
  6.5 0.0 copy-start
  6.5 0.8 copy.13
  7.4 1.9 select_reduce_fusion
  9.3 0.1 eq.59
  9.4 0.1 eq.55
  9.5 1.2 reduce-window.6
  10.7 0.2 slice_reduce_fusion
  10.9 0.1 fusion.17
  11.1 0.1 reduce_sum.34
  11.2 0.7 fusion
  11.9 35.2 %all_gather.3 = bf16[64,2048]{1,0:T(8,128)(2,1)S(1)} all-gather(bf16[8,2048]{1,0:T(8,128)(2,1)} %param.7), channel_id=1, replica_groups=mesh['ep'=64,'blk'=8] {'blk'}, dimensions={0}, use_global_device_ids=true | all-gather | bytes 294912 | tf_op jit(solution)/shard_map/all_gather | solution.py:27
  47.1 1.3 convolution_convert_fusion.1
  48.4 0.0 copy-start.2
  48.5 202.3 %all_to_all.10 = bf16[64,16,2048]{2,1,0:T(8,128)(2,1)S(1)} all-to-all(bf16[64,16,2048]{2,1,0:T(8,128)(2,1)S(1)} %bitcast.42), channel_id=1, replica_groups=mesh['ep'=64,'blk'=8] {'ep'}, dimensions={0} | all-to-all | bytes 8388608 | tf_op jit(solution)/shard_map/all_to_all | solution.py:47
  250.8 0.0 copy-start.1
  250.8 0.0 copy-start.3
  250.8 1.9 copy-done.1
  252.7 0.0 copy-done.2
  252.7 1.2 fusion.7
  254.0 0.0 copy-done
  254.0 0.0 copy-done.3
  254.0 8.5 %convolution_convert_fusion = bf16[1024,2048]{1,0:T(8,128)(2,1)} fusion(bf16[1024,2048]{1,0:T(8,128)(2,1)} %bitcast.40, bf16[1,128,2048]{2,1,0:T(8,128)(2,1)S(1)} %copy-done, bf16[1,2048,128]{2,1,0:T(8,128)(2,1)S(1)} %copy-done.3, f32[1024,128]{1,0:T(8,128)S(1)} %fusion.7), kind=kOutput, calls=%fused_computation | convolution fusion | flops 1076625408 | bytes 9961472 | tf_op jit(solution)/shard_map/dot_general | solution.py:15
  262.5 0.0 copy-start.4
  262.5 8.8 %all-to-all-start.1 = ((bf16[64,16,2048]{2,1,0:T(8,128)(2,1)}), bf16[64,16,2048]{2,1,0:T(8,128)(2,1)}, u32[]{:S(2)}, u32[]{:S(2)}) async-start(bf16[64,16,2048]{2,1,0:T(8,128)(2,1)} %bitcast.41), calls=%async_computation.1 | async-start | bytes 8388608 | tf_op jit(solution)/shard_map/all_to_all | solution.py:48
  271.3 0.0 reduce-scatter.2.cloned.1.call-start
  271.3 0.0 copy-done.4
  271.3 0.1 copy.15
  271.4 0.7 fusion.3
  272.2 183.0 %all-to-all-done.1 = bf16[64,16,2048]{2,1,0:T(8,128)(2,1)} async-done(((bf16[64,16,2048]{2,1,0:T(8,128)(2,1)}), bf16[64,16,2048]{2,1,0:T(8,128)(2,1)}, u32[]{:S(2)}, u32[]{:S(2)}) %all-to-all-start.1) | async-done | bytes 4194336 | tf_op jit(solution)/shard_map/all_to_all | solution.py:48
  455.2 3.7 convolution_convert_fusion.2
  458.9 0.0 reduce-scatter.2.cloned.1.call-update
  458.9 84.7 %reduce-scatter.2.cloned.1.call-done = bf16[8,2048]{1,0:T(8,128)(2,1)} async-done(((bf16[64,2048]{1,0:T(8,128)(2,1)}), bf16[8,2048]{1,0:T(8,128)(2,1)}) %reduce-scatter.2.cloned.1.call-update) | async-done | bytes 32784 | tf_op jit(solution)/shard_map/reduce_scatter | solution.py:55
  (4 shorter events, 0.1 us)
Async XLA Ops:
  6.5 247.4 %copy-start = (bf16[1,128,2048]{2,1,0:T(8,128)(2,1)S(1)}, bf16[1,128,2048]{2,1,0:T(8,128)(2,1)}, u32[]{:S(2)}) copy-start(bf16[1,128,2048]{2,1,0:T(8,128)(2,1)} %param.13) | copy-start | bytes 1572868
  48.4 204.3 %copy-start.2 = (bf16[1,2048,128]{2,1,0:T(8,128)(2,1)S(1)}, bf16[1,2048,128]{2,1,0:T(8,128)(2,1)}, u32[]{:S(2)}) copy-start(bf16[1,2048,128]{2,1,0:T(8,128)(2,1)} %param.11) | copy-start | bytes 1572868
  250.8 1.9 copy-start.1
  250.8 3.2 copy-start.3
  262.5 8.8 %copy-start.4 = (bf16[64,8]{0,1:T(8,128)(2,1)S(1)}, bf16[64,8]{0,1:T(8,128)(2,1)}, u32[]{:S(2)}) copy-start(bf16[64,8]{0,1:T(8,128)(2,1)} %param.9) | copy-start | bytes 3076
  262.5 192.7 %all-to-all-start.1 = ((bf16[64,16,2048]{2,1,0:T(8,128)(2,1)}), bf16[64,16,2048]{2,1,0:T(8,128)(2,1)}, u32[]{:S(2)}, u32[]{:S(2)}) async-start(bf16[64,16,2048]{2,1,0:T(8,128)(2,1)} %bitcast.41), calls=%async_computation.1 | async-start | bytes 8388608 | tf_op jit(solution)/shard_map/all_to_all | solution.py:48
  271.3 272.4 %reduce-scatter.2.cloned.1.call-start = ((), (), s32[]{:S(2)}) async-start(), calls=%async_computation.3 | async-start | bytes 294912 | tf_op jit(solution)/shard_map/reduce_scatter | solution.py:55
Sparse Core Ops, SparseCore 0:
  459.1 84.5 reduce-scatter.1
where the time goes:
time: 551 us
  waiting for transfers between devices  268 us (49%)
  blocking collectives  238 us (43%)
  matrix products  14.8 us (3%)
  between operations  13.5 us (2%)
  starting transfers between devices  8.82 us (2%)
    all_to_all x1, blocking collectives, local(): lax.all_to_all(buffer, 'ep', split_axis=0, concat_axis=0, tiled=True)  202 us
    all_to_all x1, waiting for transfers between devices, local(): lax.all_to_all(expert_rows(arrived, w_gate, w_up, w_down), 'ep', split_ax...  183 us
    reduce_scatter x1, waiting for transfers between devices, local(): lax.psum_scatter(combined.astype(jnp.bfloat16), 'blk', scatter_dimension=...  84.7 us
    all_gather x1, blocking collectives, local(): gathered = lax.all_gather(tokens, 'blk', axis=0, tiled=True)  35.2 us
  transfers between devices with their start and end apart: 2, of which 2 were waited for; matrix products, arithmetic and copies ran while one was open for 0% of the time, Pallas kernels for 0%

commit v1 on v0

--- a/solution.py
+++ b/solution.py
@@ -24,7 +24,9 @@
     block_size = own_count * blk_count
     capacity = blk_count * max(1, 2 * TOP * own_count // ep_count)
     slots_total = ep_count * capacity
-    gathered = lax.all_gather(tokens, "blk", axis=0, tiled=True)
+    gathered = jnp.concatenate(
+        lax.all_to_all(jnp.stack([tokens] * lax.axis_size("blk")), "blk", 0, 0), axis=0
+    )
     ep_ids = lax.iota(jnp.int32, ep_count)
     holder = jnp.sum(
         jnp.where(routes[:, :, None] == ep_ids[None, None, :], placement[None, None, :], 0), axis=-1

time: 551 us -> 525 us (0.953)
  blocking collectives: 238 us -> 202 us
  starting transfers between devices: 8.82 us -> 15.8 us
    all_gather x1 -> x0, blocking collectives: 35.2 us -> none  [local(): gathered = lax.all_gather(tokens, 'blk', axis=0, tiled=True)]
    all_to_all x0 -> x1, starting transfers between devices: none -> 6.93 us  [local(): lax.all_to_all(jnp.stack([tokens] * lax.axis_size('blk')), 'blk', 0, 0)]
  transfers between devices with their start and end apart: 2 -> 3, of which waited for: 2 -> 3; matrix products, arithmetic and copies ran while one was open for 0% -> 1% of each run, Pallas kernels for 0% -> 0%
where the time goes in v1:
time: 525 us
  waiting for transfers between devices  269 us (51%)
  blocking collectives  202 us (38%)
  starting transfers between devices  15.8 us (3%)
  matrix products  14.8 us (3%)
  between operations  13.5 us (3%)
    all_to_all x1, blocking collectives, local(): lax.all_to_all(buffer, 'ep', split_axis=0, concat_axis=0, tiled=True)  202 us
    all_to_all x1, waiting for transfers between devices, local(): lax.all_to_all(expert_rows(arrived, w_gate, w_up, w_down), 'ep', split_ax...  183 us
    reduce_scatter x1, waiting for transfers between devices, local(): lax.psum_scatter(combined.astype(jnp.bfloat16), 'blk', scatter_dimension=...  82.6 us
  transfers between devices with their start and end apart: 3, of which 3 were waited for; matrix products, arithmetic and copies ran while one was open for 1% of the time, Pallas kernels for 0%

profile of v1, /device:TPU:32, one launch (start us, length us, event | category | flops | bytes accessed | tf_op | source)
XLA Modules:
  0.0 524.7 jit_solution(7216064501042902869)
XLA Ops:
  6.5 0.0 copy-start
  6.5 1.5 stack.2
  8.1 6.9 %all-to-all-start = ((bf16[8,8,2048]{2,1,0:T(8,128)(2,1)}), bf16[8,8,2048]{2,1,0:T(8,128)(2,1)S(1)}, u32[]{:S(2)}, u32[]{:S(2)}) async-start(bf16[8,8,2048]{2,1,0:T(8,128)(2,1)} %stack.2), calls=%async_computation | async-start | bytes 524288 | tf_op jit(solution)/shard_map/all_to_all | solution.py:28
  15.0 0.8 copy.13
  15.8 1.9 select_reduce_fusion
  17.7 0.1 eq.59
  17.8 0.1 eq.55
  17.9 1.2 reduce-window.6
  19.1 0.2 slice_reduce_fusion
  19.3 0.1 fusion.18
  19.5 0.1 reduce_sum.34
  19.6 0.7 fusion
  20.3 3.4 all-to-all-done
  23.7 1.3 convolution_convert_fusion.1
  25.0 0.0 copy-start.2
  25.0 202.0 %all_to_all.15 = bf16[64,16,2048]{2,1,0:T(8,128)(2,1)S(1)} all-to-all(bf16[64,16,2048]{2,1,0:T(8,128)(2,1)S(1)} %bitcast.44), channel_id=1, replica_groups=mesh['ep'=64,'blk'=8] {'ep'}, dimensions={0} | all-to-all | bytes 8388608 | tf_op jit(solution)/shard_map/all_to_all | solution.py:49
  227.1 0.0 copy-start.1
  227.1 1.9 copy-done.1
  229.0 0.0 copy-done.2
  229.0 1.2 fusion.7
  230.3 0.0 copy-done
  230.3 0.0 copy-done.3
  230.3 8.5 %convolution_convert_fusion = bf16[1024,2048]{1,0:T(8,128)(2,1)} fusion(bf16[1024,2048]{1,0:T(8,128)(2,1)} %bitcast.42, bf16[1,128,2048]{2,1,0:T(8,128)(2,1)S(1)} %copy-done, bf16[1,2048,128]{2,1,0:T(8,128)(2,1)S(1)} %copy-done.3, f32[1024,128]{1,0:T(8,128)S(1)} %fusion.7), kind=kOutput, calls=%fused_computation | convolution fusion | flops 1076625408 | bytes 9961472 | tf_op jit(solution)/shard_map/dot_general | solution.py:15
  238.8 8.8 %all-to-all-start.2 = ((bf16[64,16,2048]{2,1,0:T(8,128)(2,1)}), bf16[64,16,2048]{2,1,0:T(8,128)(2,1)}, u32[]{:S(2)}, u32[]{:S(2)}) async-start(bf16[64,16,2048]{2,1,0:T(8,128)(2,1)} %bitcast.43), calls=%async_computation.2 | async-start | bytes 8388608 | tf_op jit(solution)/shard_map/all_to_all | solution.py:50
  247.6 0.0 reduce-scatter.2.cloned.1.call-start
  247.6 0.0 copy-done.4
  247.6 0.1 copy.15
  247.7 0.7 fusion.3
  248.5 183.0 %all-to-all-done.2 = bf16[64,16,2048]{2,1,0:T(8,128)(2,1)} async-done(((bf16[64,16,2048]{2,1,0:T(8,128)(2,1)}), bf16[64,16,2048]{2,1,0:T(8,128)(2,1)}, u32[]{:S(2)}, u32[]{:S(2)}) %all-to-all-start.2) | async-done | bytes 4194336 | tf_op jit(solution)/shard_map/all_to_all | solution.py:50
  431.5 3.7 convolution_convert_fusion.2
  435.2 0.0 reduce-scatter.2.cloned.1.call-update
  435.3 82.6 %reduce-scatter.2.cloned.1.call-done = bf16[8,2048]{1,0:T(8,128)(2,1)} async-done(((bf16[64,2048]{1,0:T(8,128)(2,1)}), bf16[8,2048]{1,0:T(8,128)(2,1)}) %reduce-scatter.2.cloned.1.call-update) | async-done | bytes 32784 | tf_op jit(solution)/shard_map/reduce_scatter | solution.py:57
  (6 shorter events, 0.1 us)
Async XLA Ops:
  6.5 223.7 %copy-start = (bf16[1,128,2048]{2,1,0:T(8,128)(2,1)S(1)}, bf16[1,128,2048]{2,1,0:T(8,128)(2,1)}, u32[]{:S(2)}) copy-start(bf16[1,128,2048]{2,1,0:T(8,128)(2,1)} %param.13) | copy-start | bytes 1572868
  8.1 15.7 %all-to-all-start = ((bf16[8,8,2048]{2,1,0:T(8,128)(2,1)}), bf16[8,8,2048]{2,1,0:T(8,128)(2,1)S(1)}, u32[]{:S(2)}, u32[]{:S(2)}) async-start(bf16[8,8,2048]{2,1,0:T(8,128)(2,1)} %stack.2), calls=%async_computation | async-start | bytes 524288 | tf_op jit(solution)/shard_map/all_to_all | solution.py:28
  25.0 204.0 %copy-start.2 = (bf16[1,2048,128]{2,1,0:T(8,128)(2,1)S(1)}, bf16[1,2048,128]{2,1,0:T(8,128)(2,1)}, u32[]{:S(2)}) copy-start(bf16[1,2048,128]{2,1,0:T(8,128)(2,1)} %param.11) | copy-start | bytes 1572868
  227.1 1.9 copy-start.1
  227.1 3.2 copy-start.3
  238.8 8.8 %copy-start.4 = (bf16[64,8]{0,1:T(8,128)(2,1)S(1)}, bf16[64,8]{0,1:T(8,128)(2,1)}, u32[]{:S(2)}) copy-start(bf16[64,8]{0,1:T(8,128)(2,1)} %param.9) | copy-start | bytes 3076
  238.8 192.7 %all-to-all-start.2 = ((bf16[64,16,2048]{2,1,0:T(8,128)(2,1)}), bf16[64,16,2048]{2,1,0:T(8,128)(2,1)}, u32[]{:S(2)}, u32[]{:S(2)}) async-start(bf16[64,16,2048]{2,1,0:T(8,128)(2,1)} %bitcast.43), calls=%async_computation.2 | async-start | bytes 8388608 | tf_op jit(solution)/shard_map/all_to_all | solution.py:50
  247.6 270.3 %reduce-scatter.2.cloned.1.call-start = ((), (), s32[]{:S(2)}) async-start(), calls=%async_computation.4 | async-start | bytes 294912 | tf_op jit(solution)/shard_map/reduce_scatter | solution.py:57
Sparse Core Ops, SparseCore 0:
  435.4 82.4 reduce-scatter.1
